TPU v7x, 256 devices: a whole 4x4x8 slice. The times are simulated.
256 devices in a mesh: enc: 4 (over z_lo), lab: 64 (over z_hi, y, x, core).
Axes of the slice: x: 4, y: 4, z: 8 (z_hi: 2, z_lo: 4; z = z_hi * 4 + z_lo), core: 2. Of those that a mesh axis runs over, the one named last changes fastest.
Arguments:
- embeddings: bfloat16 [131072, 768], P(('enc', 'lab')), may hold values from -6 to 6
- classifier: float32 [4096, 768], P('lab'), may hold values from -0.21875 to 0.21875
- label_valid: int32 [4096], P('lab'), may hold values 0 or 1
- shortlist: int32 [131072, 4], P(('enc', 'lab')), may hold values from 0 to 63, all different within a row; in each aligned block of 512 rows (0 to 511, 512 to 1023, ...) at most 48 rows name the same one
- slot_live: int32 [131072, 4], P(('enc', 'lab')), may hold values 0 or 1
- positive: int32 [131072, 4], P(('enc', 'lab')), may hold values from 0 to 63
- negative: int32 [131072, 4, 8], P(('enc', 'lab')), may hold values from 0 to 63
Outputs:
- w_grad: float32 [4096, 768], P('lab')
- emb_grad: float32 [131072, 768], P(('enc', 'lab'))
Inputs may be any that keep to these rules, and one draw needn't show every extreme that they name: `shortlist`: each document names 4 different clusters; among the 512 documents of one device no cluster is named by more than 48 documents.
All inputs are finite; a program needn't handle non-finite values. No bound on the sum of `label_valid` or of `slot_live` on one device may be relied on, other than what follows from the above.
Results may differ from a plain program's by a relative error of at most 0.0041.
Values may be sent and summed in bfloat16 or wider, within the bound.
A program may use at most 128 MiB of HBM per device.

v0:
```python
import math

import jax
import jax.numpy as jnp
from jax import lax
from jax.sharding import PartitionSpec as P


def dense_targets(shortlist, slot_live, positive, negative, clusters, panel):
    labels = jnp.arange(panel, dtype=jnp.int32)
    pos_hot = (positive[..., None] == labels).astype(jnp.float32)
    neg_count = jnp.sum((negative[..., None] == labels).astype(jnp.float32), axis=2)
    live = slot_live.astype(jnp.float32)[..., None]
    slot_weight = live * (pos_hot + neg_count)
    cluster_hot = (shortlist[..., None] == jnp.arange(clusters, dtype=jnp.int32)).astype(
        jnp.float32
    )
    count = shortlist.shape[0]
    weight = jnp.einsum("nsc,nsj->ncj", cluster_hot, slot_weight).reshape(count, clusters * panel)
    target = jnp.einsum("nsc,nsj->ncj", cluster_hot, pos_hot).reshape(count, clusters * panel)
    return (weight.astype(jnp.bfloat16), target.astype(jnp.bfloat16))


def make_absorb(embeddings, weight_all, target_all):

    def absorb(carry, pieces, start):
        w_piece, v_piece = pieces
        weight = weight_all.astype(jnp.float32)
        weight = weight * v_piece.astype(jnp.float32)[None, :]
        target = target_all.astype(jnp.float32)
        logits = lax.dot_general(
            embeddings, w_piece, (((1,), (1,)), ((), ())), preferred_element_type=jnp.float32
        )
        dlogits = (weight * (jax.nn.sigmoid(logits) - target)).astype(jnp.bfloat16)
        grad_acc = jnp.dot(dlogits, w_piece, preferred_element_type=jnp.float32)
        return (grad_acc, dlogits)

    return absorb


def shards(embeddings, classifier, label_valid, shortlist, slot_live, positive, negative):
    lab_count = lax.axis_size("lab")
    enc_count = lax.axis_size("enc")
    docs, width = embeddings.shape
    panel = classifier.shape[0]
    slots = shortlist.shape[1]
    classifier_b = classifier.astype(jnp.bfloat16)
    weight_all, target_all = dense_targets(
        shortlist, slot_live, positive, negative, lab_count, panel
    )
    absorb = make_absorb(embeddings, weight_all, target_all)
    initial = (
        jnp.zeros((docs, width), jnp.float32),
        jnp.zeros((docs, lab_count * panel), jnp.bfloat16),
    )
    emb_grad, scored = absorb(
        initial,
        (
            lax.all_gather(classifier_b, "lab", axis=0, tiled=True),
            lax.all_gather(label_valid.astype(jnp.bfloat16), "lab", axis=0, tiled=True),
        ),
        jnp.int32(0),
    )
    partial_grad = lax.psum_scatter(
        lax.dot_general(
            scored, embeddings, (((0,), (0,)), ((), ())), preferred_element_type=jnp.float32
        ),
        "lab",
        scatter_dimension=0,
        tiled=True,
    )
    scale_factor = 1.0 / math.sqrt(docs * enc_count * slots)
    w_grad = lax.psum(partial_grad, "enc") * scale_factor
    return (w_grad, emb_grad)


def solution(mesh):
    in_specs = (
        P(("enc", "lab"), None),
        P("lab", None),
        P("lab"),
        P(("enc", "lab"), None),
        P(("enc", "lab"), None),
        P(("enc", "lab"), None),
        P(("enc", "lab"), None, None),
    )
    out_specs = (P("lab", None), P(("enc", "lab"), None))
    return jax.shard_map(shards, mesh=mesh, in_specs=in_specs, out_specs=out_specs, check_vma=False)
```

profile of v0, /device:TPU:32, one launch (start us, length us, event | category | flops | bytes accessed | tf_op | source)
XLA Modules:
  0.0 584.3 jit_solution(4797817930439539385)
XLA Ops:
  7.2 1.6 convert_element_type.50
  8.9 0.8 copy.21
  9.8 0.7 convert_element_type.42
  10.5 1.4 convert_reduce_fusion
  11.9 0.8 add_multiply_fusion
  12.7 0.3 copy.22
  13.0 8.6 %convert_convert_fusion.1 = f32[512,64,64]{2,1,0:T(8,128)} fusion(bf16[512,4,64]{2,1,0:T(4,128)(2,1)S(1)} %copy.22, s32[512,4]{1,0:T(8,128)S(1)} %copy.21), kind=kOutput, calls=%fused_computation.2 | convolution fusion | flops 19005440 | bytes 8658944 | tf_op jit(solution)/shard_map/nsc,nsj->ncj/dot_general | solution.py:19
  21.6 12.8 %copy.23 = f32[512,64,64]{0,2,1:T(8,128)} copy(f32[512,64,64]{2,1,0:T(8,128)} %convert_convert_fusion.1) | data formatting | bytes 16777216 | tf_op jit(solution)/shard_map/convert_element_type | solution.py:28
  34.4 8.9 %copy.24 = f32[512,4096]{1,0:T(8,128)} copy(f32[512,4096]{0,1:T(8,128)} %bitcast.11) | data formatting | bytes 16777216 | tf_op jit(solution)/shard_map/convert_element_type | solution.py:28
  43.3 0.1 iota_compare_fusion.4
  43.4 0.4 copy.25
  43.9 8.7 %convert_convert_fusion = f32[512,64,64]{2,1,0:T(8,128)} fusion(pred[512,4,64]{2,1,0:T(4,128)(4,1)S(1)} %copy.25, s32[512,4]{1,0:T(8,128)S(1)} %copy.21), kind=kOutput, calls=%fused_computation.1 | convolution fusion | flops 21102592 | bytes 8527872 | tf_op jit(solution)/shard_map/nsc,nsj->ncj/dot_general | solution.py:20
  52.5 12.8 %copy.26 = f32[512,64,64]{0,2,1:T(8,128)} copy(f32[512,64,64]{2,1,0:T(8,128)} %convert_convert_fusion) | data formatting | bytes 16777216 | tf_op jit(solution)/shard_map/convert_element_type | solution.py:30
  65.3 9.0 %copy.27 = f32[512,4096]{1,0:T(8,128)} copy(f32[512,4096]{0,1:T(8,128)} %bitcast.12) | data formatting | bytes 16777216 | tf_op jit(solution)/shard_map/convert_element_type | solution.py:30
  74.3 0.6 dynamic-slice
  75.6 0.2 dynamic-update-slice
  75.8 215.7 %all-reduce = bf16[4096]{0:T(1024)(128)(2,1)S(1)} all-reduce(bf16[4096]{0:T(1024)(128)(2,1)S(1)} %dynamic-update-slice), channel_id=1, replica_groups=mesh['enc'=4,'lab'=64] {'lab'}, use_global_device_ids=true, to_apply=%add | all-reduce | flops 4096 | bytes 16384
  291.6 11.0 %multiply_convert_fusion = bf16[512,4096]{1,0:T(8,128)(2,1)} fusion(f32[512,4096]{1,0:T(8,128)} %copy.27, f32[512,4096]{1,0:T(8,128)} %copy.24, bf16[512,768]{1,0:T(8,128)(2,1)S(1)} %copy-done, bf16[4096,768]{1,0:T(8,128)(2,1)} %all-gather.2.cloned.1.call-done, f32[4096]{0:T(1024)S(1)} %convert_element_type.49), kind=kOutput, calls=%fused_computation | convolution fusion | flops 3235905536 | bytes 28065792 | tf_op jit(solution)/shard_map/dot_general | solution.py:31
  302.6 10.2 %fusion.2 = f32[4096,768]{1,0:T(8,128)} fusion(bf16[512,4096]{1,0:T(8,128)(2,1)} %multiply_convert_fusion, bf16[512,768]{1,0:T(8,128)(2,1)S(1)} %copy-done), kind=kOutput, calls=%fused_computation.11 | convolution fusion | flops 3221225472 | bytes 17563648 | tf_op jit(solution)/shard_map/dot_general | solution.py:65
  312.8 0.0 all-reduce.3.cloned.1.call-start
  312.9 218.0 %reduce-scatter.2.cloned.1.call-done = f32[64,768]{1,0:T(8,128)} async-done(((f32[4096,768]{1,0:T(8,128)}), f32[64,768]{1,0:T(8,128)}) %reduce-scatter.2.cloned.1.call-update) | async-done | bytes 196624 | tf_op jit(solution)/shard_map/reduce_scatter | solution.py:64
  530.9 8.6 %fusion.3 = f32[512,768]{1,0:T(8,128)} fusion(bf16[512,4096]{1,0:T(8,128)(2,1)} %multiply_convert_fusion, bf16[4096,768]{1,0:T(8,128)(2,1)} %all-gather.2.cloned.1.call-done), kind=kOutput, calls=%fused_computation.12 | convolution fusion | flops 3221225472 | bytes 12058624 | tf_op jit(solution)/shard_map/dot_general | solution.py:35
  539.5 36.7 %all-reduce.3.cloned.1.call-done = f32[64,768]{1,0:T(8,128)} async-done(((f32[64,768]{1,0:T(8,128)}), f32[64,768]{1,0:T(8,128)}) %all-reduce.3.cloned.1.call-update) | async-done | bytes 196624 | tf_op jit(solution)/shard_map/psum | solution.py:73
  576.2 1.6 broadcast_multiply_fusion
  (17 shorter events, 0.2 us)
Async XLA Ops:
  7.2 284.4 %copy-start = (bf16[512,768]{1,0:T(8,128)(2,1)S(1)}, bf16[512,768]{1,0:T(8,128)(2,1)}, u32[]{:S(2)}) copy-start(bf16[512,768]{1,0:T(8,128)(2,1)} %param.7) | copy-start | bytes 2359300
  7.2 284.4 %all-gather.2.cloned.1.call-start = ((), (), s32[]{:S(2)}) async-start(), calls=%async_computation.1 | async-start | bytes 6389760 | tf_op jit(solution)/shard_map/all_gather | solution.py:59
  8.9 522.0 %reduce-scatter.2.cloned.1.call-start = ((), (), s32[]{:S(2)}) async-start(), calls=%async_computation.2 | async-start | bytes 12779520 | tf_op jit(solution)/shard_map/reduce_scatter | solution.py:64
  34.4 9.0 %copy-start.1 = (s32[512,4]{0,1:T(4,128)S(1)}, s32[512,4]{0,1:T(4,128)}, u32[]{:S(2)}) copy-start(s32[512,4]{0,1:T(4,128)} %param.12) | copy-start | bytes 24580
  65.3 9.0 %copy-start.2 = (s32[64]{0:T(128)S(1)}, s32[64]{0:T(128)}, u32[]{:S(2)}) copy-start(s32[64]{0:T(128)} %param.9) | copy-start | bytes 772
  65.3 9.0 %copy-start.3 = (u32[256]{0:T(256)S(1)}, u32[256]{0:T(256)}, u32[]{:S(2)}) copy-start(u32[256]{0:T(256)} %constant.8) | copy-start | bytes 3076
  312.8 263.4 %all-reduce.3.cloned.1.call-start = ((), (), s32[]{:S(2)}) async-start(), calls=%async_computation.3 | async-start | bytes 393216 | tf_op jit(solution)/shard_map/psum | solution.py:73
Sparse Core Ops, SparseCore 0:
  12.3 104.5 all-gather.1
  312.9 217.9 reduce-scatter.1
  533.5 42.6 all-reduce.2
where the time goes:
time: 588 us; the launch traced here: 584 us
  waiting for transfers between devices  255 us (43%)
  blocking collectives  216 us (37%)
  matrix products  47 us (8%)
  local copies, waits for them, and re-layouts  46 us (8%)
  between operations  14.5 us (2%)
  other arithmetic  6.25 us (1%)
    reduce_scatter x1, waiting for transfers between devices, shards(): lax.psum_scatter(lax.dot_general(scored, embeddings, (((0,), (0,)), ((),...  218 us
    unnamed x1, blocking collectives  216 us
    psum x1, waiting for transfers between devices, shards(): w_grad = lax.psum(partial_grad, 'enc') * scale_factor  36.7 us
    convert_element_type x2, local copies, waits for them, and re-layouts, absorb(): target = target_all.astype(jnp.float32)  21.8 us
    convert_element_type x2, local copies, waits for them, and re-layouts, absorb(): weight = weight_all.astype(jnp.float32)  21.7 us
  transfers between devices with their start and end apart: 3, of which 2 were waited for; matrix products, arithmetic and copies ran while one was open for 13% of the time, Pallas kernels for 0%

commit v1 on v0

v1 whole, which is shorter than its diff:
```python
import functools
import math

import jax
import jax.numpy as jnp
from jax import lax
from jax.experimental import pallas as pl
from jax.experimental.pallas import tpu as pltpu
from jax.sharding import PartitionSpec as P

MESH = pl.DeviceIdType.MESH
NT = (((1,), (1,)), ((), ()))
TN = (((0,), (0,)), ((), ()))


def rem4(v):
    return lax.rem(v + 8, 4)


class Place:
    def __init__(self):
        self.e = lax.axis_index("enc")
        lab = lax.axis_index("lab")
        self.c = lax.rem(lab, 2)
        self.x = lax.rem(lax.div(lab, 2), 4)
        self.y = lax.rem(lax.div(lab, 8), 4)
        self.h = lax.div(lab, 32)
        self.z = self.h * 4 + self.e

    def lab_of(self, h, y, x, c):
        return ((h * 4 + y) * 4 + x) * 2 + c

    def along_x(self, k):
        return (self.e, self.lab_of(self.h, self.y, rem4(self.x + k), self.c))

    def along_y(self, k):
        return (self.e, self.lab_of(self.h, rem4(self.y + k), self.x, self.c))

    def sibling(self):
        return (self.e, self.lab_of(self.h, self.y, self.x, 1 - self.c))

    def mirror(self):
        return (3 - self.e, self.lab_of(1 - self.h, self.y, self.x, self.c))

    def z_of(self, k):
        return lax.rem(self.z + k, 8)

    def along_z(self, k):
        z = self.z_of(k)
        return (lax.rem(z, 4), self.lab_of(lax.div(z, 4), self.y, self.x, self.c))

    def along_enc(self, k):
        return (rem4(self.e + k), self.lab_of(self.h, self.y, self.x, self.c))


class Mail:
    def __init__(self, send, recv):
        self.send, self.recv, self.used, self.sent = send, recv, 0, []

    def post(self, src, dst, device):
        n = self.used
        self.used += 1
        copy = pltpu.make_async_remote_copy(
            src_ref=src,
            dst_ref=dst,
            send_sem=self.send.at[n],
            recv_sem=self.recv.at[n],
            device_id=device,
            device_id_type=MESH,
        )
        copy.start()
        self.sent.append(copy)
        return copy

    def finish(self):
        for copy in self.sent:
            copy.wait_send()


def gather_half(mail, at, own, rh):
    block = lambda ry, rx: own.at[rh, ry, rx]
    right, left, up, down = at.along_x(1), at.along_x(-1), at.along_y(1), at.along_y(-1)
    post = mail.post
    xr = post(block(0, 0), block(0, 3), right)
    yu = post(block(0, 0), block(3, 0), up)
    xl = post(block(0, 0), block(0, 1), left)
    yd = post(block(0, 0), block(1, 0), down)
    yield
    half = lambda ry, rx, k: own.at[rh, ry, rx, k]
    sub = lambda ry, rx, k: own.at[rh, ry, rx, :, k]
    quarter = lambda ry, rx, k, s: own.at[rh, ry, rx, k, s]
    xr.wait_recv()
    x2a = post(sub(0, 3, 0), sub(0, 2, 0), right)
    u3 = post(half(0, 3, 0), half(3, 3, 0), up)
    d3 = post(half(0, 3, 0), half(1, 3, 0), down)
    yield
    yu.wait_recv()
    y2a = post(sub(3, 0, 0), sub(2, 0, 0), up)
    r3 = post(half(3, 0, 1), half(3, 3, 1), right)
    l3 = post(half(3, 0, 1), half(3, 1, 1), left)
    yield
    xl.wait_recv()
    x2b = post(sub(0, 1, 1), sub(0, 2, 1), left)
    u1 = post(half(0, 1, 0), half(3, 1, 0), up)
    d1 = post(half(0, 1, 0), half(1, 1, 0), down)
    yield
    yd.wait_recv()
    y2b = post(sub(1, 0, 1), sub(2, 0, 1), down)
    r1 = post(half(1, 0, 1), half(1, 3, 1), right)
    l1 = post(half(1, 0, 1), half(1, 1, 1), left)
    yield
    x2a.wait_recv()
    x2b.wait_recv()
    u2 = post(half(0, 2, 0), half(3, 2, 0), up)
    d2 = post(half(0, 2, 0), half(1, 2, 0), down)
    y2a.wait_recv()
    y2b.wait_recv()
    r2 = post(half(2, 0, 1), half(2, 3, 1), right)
    l2 = post(half(2, 0, 1), half(2, 1, 1), left)
    yield
    last = []
    for rx, u in ((3, u3), (1, u1)):
        u.wait_recv()
        last.append(post(quarter(3, rx, 0, 0), quarter(2, rx, 0, 0), up))
    for ry, r in ((3, r3), (1, r1)):
        r.wait_recv()
        last.append(post(quarter(ry, 3, 1, 0), quarter(ry, 2, 1, 0), right))
    for rx, d in ((3, d3), (1, d1)):
        d.wait_recv()
        last.append(post(quarter(1, rx, 0, 1), quarter(2, rx, 0, 1), down))
    for ry, l in ((3, l3), (1, l1)):
        l.wait_recv()
        last.append(post(quarter(ry, 1, 1, 1), quarter(ry, 2, 1, 1), left))
    yield
    u2.wait_recv()
    last.append(post(quarter(3, 2, 0, 0), quarter(2, 2, 0, 0), up))
    r2.wait_recv()
    last.append(post(quarter(2, 3, 1, 0), quarter(2, 2, 1, 0), right))
    d2.wait_recv()
    last.append(post(quarter(1, 2, 0, 1), quarter(2, 2, 0, 1), down))
    l2.wait_recv()
    last.append(post(quarter(2, 1, 1, 1), quarter(2, 2, 1, 1), left))
    yield
    for copy in last:
        copy.wait_recv()


class RingSum:
    def __init__(self, mail, send, recv, groups, value, plus, minus):
        self.mail, self.out, self.into, self.groups, self.value = mail, send, recv, groups, value
        self.plus, self.minus = plus, minus
        self.copies = {}

    def fill(self, way, slot, make):
        def one(g, carry):
            self.out[way, slot, g] = make(g).astype(jnp.bfloat16)
            return carry

        lax.fori_loop(0, self.groups, one, 0)
        self.copies[way, slot] = self.mail.post(
            self.out.at[way, slot], self.into.at[way, slot], self.plus if way == 0 else self.minus
        )

    def far(self):
        self.fill(0, 0, lambda g: self.value(g, 2, 0))
        self.fill(1, 0, lambda g: self.value(g, 2, 1))

    def near(self):
        self.fill(0, 1, lambda g: self.value(g, 1, 1))
        self.fill(1, 1, lambda g: self.value(g, 3, 0))

    def got(self, way, slot, g):
        return self.into[way, slot, g].astype(jnp.float32)

    def relay(self):
        self.copies[0, 0].wait_recv()
        self.fill(0, 2, lambda g: self.value(g, 1, 0) + self.got(0, 0, g))
        self.copies[1, 0].wait_recv()
        self.fill(1, 2, lambda g: self.value(g, 3, 1) + self.got(1, 0, g))

    def collect(self, store):
        for way in (0, 1):
            for slot in (1, 2):
                self.copies[way, slot].wait_recv()

        def one(g, carry):
            store(g, 0, self.value(g, 0, 0) + self.got(0, 2, g) + self.got(1, 1, g))
            store(g, 1, self.value(g, 0, 1) + self.got(0, 1, g) + self.got(1, 2, g))
            return carry

        lax.fori_loop(0, self.groups, one, 0)


def slot_weights(short_ref, live_ref, pos_ref, neg_ref, sw, panel, slots, nneg):
    docs = pos_ref.shape[1]
    label = lax.broadcasted_iota(jnp.int32, (panel, docs), 0)
    for s in range(slots):
        hot = jnp.where(pos_ref[pl.ds(s, 1), :] == label, 1.0, 0.0)
        count = hot
        for k in range(nneg):
            count += jnp.where(neg_ref[pl.ds(s * nneg + k, 1), :] == label, 1.0, 0.0)
        half = 0.5 * live_ref[pl.ds(s, 1), :].astype(jnp.float32)
        sw[s] = half * count * (1.0 - 2.0 * hot)


def kernel(
    scale, panel, slots, nneg,
    emb_ref, cls_ref, valid_ref, short_ref, live_ref, pos_ref, neg_ref,
    wg_ref, eg_ref,
    G, embh, sw, K, sib_out, sib_in,
    a1_out, a1_in, b1_out, b1_in, sum_a, sum_b, a2_out, a2_in, b2_out, b2_in,
    V, z_out, z_in, part,
    send, recv, sib_send, sib_recv,
):
    at = Place()
    width = emb_ref.shape[1]
    barrier = pltpu.get_barrier_semaphore()
    partners = [at.along_x(1), at.along_x(-1), at.along_y(1), at.along_y(-1), at.sibling()]
    partners += [at.along_z(k) for k in range(1, 8)]
    for device in partners:
        pl.semaphore_signal(barrier, inc=1, device_id=device, device_id_type=MESH)

    rows = lax.broadcasted_iota(jnp.int32, (panel, panel), 0)
    cols = lax.broadcasted_iota(jnp.int32, (panel, panel), 1)
    flags = jnp.where(rows == cols, valid_ref[...].astype(jnp.float32), 0.0)
    valid = jnp.sum(flags, axis=1, keepdims=True)
    mine = (cls_ref[...] * valid).astype(jnp.bfloat16)
    G[0, 0, 0, 0] = mine.reshape(2, 2, 16, width)
    pl.semaphore_wait(barrier, len(partners))

    mail = Mail(send, recv)
    own = G.at[0]
    mirrored = mail.post(own.at[0, 0, 0], own.at[1, 0, 0], at.mirror())
    near = gather_half(mail, at, own, 0)
    next(near)
    embh[...] = emb_ref[...] * jnp.bfloat16(0.5)
    slot_weights(short_ref, live_ref, pos_ref, neg_ref, sw, panel, slots, nneg)
    for _ in range(4):
        next(near)
    mirrored.wait_recv()
    other = gather_half(mail, at, own, 1)
    next(other)
    to_sibling = []

    def hand_over(rh, first, last):
        to_sibling.append(
            mail.post(G.at[0, rh, pl.ds(first, last - first)], G.at[1, rh, pl.ds(first, last - first)], at.sibling())
        )

    for _ in near:
        next(other, None)
    hand_over(0, 0, 4)
    for _ in other:
        pass
    hand_over(1, 0, 4)
    for copy in to_sibling:
        copy.wait_recv()

    eg_ref[...] = jnp.zeros_like(eg_ref)

    def score(rc, g):
        rh, ry = lax.div(g, 4), lax.rem(g, 4)
        w = G[rc, rh, ry].reshape(4 * panel, width)
        half_logits = lax.dot_general(w, embh[...], NT, preferred_element_type=jnp.float32)
        c = at.c if rc == 0 else 1 - at.c
        h = lax.rem(at.h + rh, 2)
        y = lax.rem(at.y + ry, 4)
        pieces = []
        for rx in range(4):
            cluster = at.lab_of(h, y, rem4(at.x + rx), c)
            hw = None
            for s in range(slots):
                term = sw[s] * jnp.where(short_ref[pl.ds(s, 1), :] == cluster, 1.0, 0.0)
                hw = term if hw is None else hw + term
            t = jnp.tanh(half_logits[rx * panel : (rx + 1) * panel])
            pieces.append((jnp.abs(hw) * t + hw).astype(jnp.bfloat16))
        dl = jnp.concatenate(pieces, axis=0)
        eg_ref[...] += lax.dot_general(dl, w, TN, preferred_element_type=jnp.float32)
        grad = jnp.dot(dl, emb_ref[...], preferred_element_type=jnp.float32)
        return rh, ry, grad.reshape(4, 2, 2, 16, width)

    def sibling_copy(g):
        rh, ry = lax.div(g, 4), lax.rem(g, 4)
        return pltpu.make_async_remote_copy(
            src_ref=sib_out.at[rh, ry],
            dst_ref=sib_in.at[rh, ry],
            send_sem=sib_send.at[g],
            recv_sem=sib_recv.at[g],
            device_id=at.sibling(),
            device_id_type=MESH,
        )

    def for_sibling(g, carry):
        rh, ry, grad = score(1, g)
        sib_out[rh, ry] = grad.astype(jnp.bfloat16)
        sibling_copy(g).start()
        return carry

    lax.fori_loop(0, 8, for_sibling, 0)

    def for_own(g, carry):
        rh, ry, grad = score(0, g)
        sibling_copy(g).wait_recv()
        K[rh, ry] = grad + sib_in[rh, ry].astype(jnp.float32)
        return carry

    lax.fori_loop(0, 8, for_own, 0)

    right, left, up, down = at.along_x(1), at.along_x(-1), at.along_y(1), at.along_y(-1)
    a1 = RingSum(
        mail, a1_out, a1_in, 8, lambda g, rel, s: K[lax.div(g, 4), lax.rem(g, 4), rel, 0, s], right, left
    )
    b1 = RingSum(
        mail, b1_out, b1_in, 8, lambda g, rel, s: K[lax.div(g, 4), rel, lax.rem(g, 4), 1, s], up, down
    )
    a1.far()
    b1.far()
    a1.near()
    b1.near()
    a1.relay()
    b1.relay()

    def store_a(g, s, v):
        sum_a[lax.div(g, 4), lax.rem(g, 4), s] = v

    def store_b(g, s, v):
        sum_b[lax.div(g, 4), lax.rem(g, 4), s] = v

    a1.collect(store_a)
    a2 = RingSum(mail, a2_out, a2_in, 2, lambda g, rel, s: sum_a[g, rel, s], up, down)
    a2.far()
    b1.collect(store_b)
    b2 = RingSum(mail, b2_out, b2_in, 2, lambda g, rel, s: sum_b[g, rel, s], right, left)
    b2.far()
    a2.near()
    b2.near()
    a2.relay()
    b2.relay()

    def store_va(g, s, v):
        V[g, s] = v
        z_out[g, s] = v.astype(jnp.bfloat16)

    def store_vb(g, s, v):
        V[g, 2 + s] = v
        z_out[g, 2 + s] = v.astype(jnp.bfloat16)

    a2.collect(store_va)
    b2.collect(store_vb)

    slices = []
    for k in range(1, 8):
        z = at.z_of(k)
        side = lax.rem(lax.div(z, 4) + at.h, 2)
        slices.append(mail.post(z_out.at[side, lax.rem(z, 4)], z_in.at[k - 1], at.along_z(k)))
    total = V[0, at.e]
    for k in range(1, 8):
        slices[k - 1].wait_recv()
        total += z_in[k - 1].astype(jnp.float32)
    part[at.e] = total * scale
    shares = [mail.post(part.at[at.e], part.at[at.e], at.along_enc(k)) for k in range(1, 4)]
    for copy in shares:
        copy.wait_recv()
    wg_ref[...] = part[...].reshape(panel, width) * valid

    mail.finish()

    def drain(g, carry):
        sibling_copy(g).wait_send()
        return carry

    lax.fori_loop(0, 8, drain, 0)


def shards(embeddings, classifier, label_valid, shortlist, slot_live, positive, negative):
    lab_count = lax.axis_size("lab")
    enc_count = lax.axis_size("enc")
    docs, width = embeddings.shape
    panel = classifier.shape[0]
    slots = shortlist.shape[1]
    nneg = negative.shape[2]
    scale = 1.0 / math.sqrt(docs * enc_count * slots)
    by_slot = lambda a: a.transpose(1, 0)
    vmem = pl.BlockSpec(memory_space=pltpu.VMEM)
    bf16, f32 = jnp.bfloat16, jnp.float32
    piece = (16, width)
    return pl.pallas_call(
        functools.partial(kernel, scale, panel, slots, nneg),
        out_shape=(
            jax.ShapeDtypeStruct((panel, width), f32),
            jax.ShapeDtypeStruct((docs, width), f32),
        ),
        in_specs=[vmem] * 7,
        out_specs=(vmem, vmem),
        scratch_shapes=[
            pltpu.VMEM((2, 2, 4, 4, 2, 2) + piece, bf16),
            pltpu.VMEM((docs, width), bf16),
            pltpu.VMEM((slots, panel, docs), f32),
            pltpu.VMEM((2, 4, 4, 2, 2) + piece, f32),
            pltpu.VMEM((2, 4, 4, 2, 2) + piece, bf16),
            pltpu.VMEM((2, 4, 4, 2, 2) + piece, bf16),
            pltpu.VMEM((2, 3, 8) + piece, bf16),
            pltpu.VMEM((2, 3, 8) + piece, bf16),
            pltpu.VMEM((2, 3, 8) + piece, bf16),
            pltpu.VMEM((2, 3, 8) + piece, bf16),
            pltpu.VMEM((2, 4, 2) + piece, f32),
            pltpu.VMEM((2, 4, 2) + piece, f32),
            pltpu.VMEM((2, 3, 2) + piece, bf16),
            pltpu.VMEM((2, 3, 2) + piece, bf16),
            pltpu.VMEM((2, 3, 2) + piece, bf16),
            pltpu.VMEM((2, 3, 2) + piece, bf16),
            pltpu.VMEM((2, 4) + piece, f32),
            pltpu.VMEM((2, 4) + piece, bf16),
            pltpu.VMEM((7,) + piece, bf16),
            pltpu.VMEM((4,) + piece, f32),
            pltpu.SemaphoreType.DMA((104,)),
            pltpu.SemaphoreType.DMA((104,)),
            pltpu.SemaphoreType.DMA((8,)),
            pltpu.SemaphoreType.DMA((8,)),
        ],
        compiler_params=pltpu.CompilerParams(
            collective_id=0, has_side_effects=True, vmem_limit_bytes=60 * 1024 * 1024
        ),
        name="step",
    )(
        embeddings,
        classifier,
        label_valid.reshape(1, panel),
        by_slot(shortlist),
        by_slot(slot_live),
        by_slot(positive),
        negative.transpose(1, 2, 0).reshape(slots * nneg, docs),
    )


def solution(mesh):
    in_specs = (
        P(("enc", "lab"), None),
        P("lab", None),
        P("lab"),
        P(("enc", "lab"), None),
        P(("enc", "lab"), None),
        P(("enc", "lab"), None),
        P(("enc", "lab"), None, None),
    )
    out_specs = (P("lab", None), P(("enc", "lab"), None))
    return jax.shard_map(shards, mesh=mesh, in_specs=in_specs, out_specs=out_specs, check_vma=False)
```

time: 588 us -> 98 us (0.17)
  waiting for transfers between devices: 255 us -> 0 us
  blocking collectives: 216 us -> 0 us
  Pallas kernels: 0 us -> 91.6 us
  matrix products: 47 us -> 0 us
  local copies, waits for them, and re-layouts: 46 us -> 4.27 us
  between operations: 14.5 us -> 0.64 us
  other arithmetic: 6.25 us -> 0 us
    reduce_scatter x1 -> x0, waiting for transfers between devices: 218 us -> none  [shards(): lax.psum_scatter(lax.dot_general(scored, embeddings, (((0,), (0,)), ((),...]
    unnamed x1 -> x0, blocking collectives: 216 us -> none
    pallas_call x0 -> x1, Pallas kernels: none -> 91.6 us  [shards(): pl.pallas_call(functools.partial(kernel, scale, panel, slots, nneg), out_...]
    dot_general x5 -> x0, matrix products: 47 us -> none  [the longest x1 11 us: absorb(): lax.dot_general(embeddings, w_piece, (((1,), (1,)), ((), ())), preferred_...]
    convert_element_type x4 -> x0, local copies, waits for them, and re-layouts: 43.5 us -> none  [the longest x2 21.8 us: absorb(): target = target_all.astype(jnp.float32)]
    psum x1 -> x0, waiting for transfers between devices: 36.7 us -> none  [shards(): w_grad = lax.psum(partial_grad, 'enc') * scale_factor]
  transfers between devices with their start and end apart: 3 -> 0, of which waited for: 2 -> 0; matrix products, arithmetic and copies ran while one was open for 13% -> 0% of each run, Pallas kernels for 0% -> 0%
where the time goes in v1:
time: 98 us; the launch traced here: 96.5 us
  Pallas kernels  91.6 us (93%)
  local copies, waits for them, and re-layouts  4.27 us (4%)
    pallas_call x1, Pallas kernels, shards(): pl.pallas_call(functools.partial(kernel, scale, panel, slots, nneg), out_...  91.6 us
    unnamed x2, local copies, waits for them, and re-layouts  4.27 us

profile of v1, /device:TPU:32, one launch (start us, length us, event | category | flops | bytes accessed | tf_op | source)
XLA Modules:
  0.0 96.5 jit_solution(8264720987153678560)
XLA Ops:
  0.6 91.6 %step.1 = (f32[64,768]{1,0:T(8,128)}, f32[512,768]{1,0:T(8,128)}) custom-call(bf16[512,768]{1,0:T(8,128)(2,1)} %emb_ref.1, f32[64,768]{1,0:T(8,128)} %cls_ref.1, s32[1,64]{1,0:T(1,128)} %bitcast.11, s32[4,512]{1,0:T(4,128)} %bitcast.8, s32[4,512]{1,0:T(4,128)} %bitcast.9, s32[4,512]{1,0:T(4,128)} %bitcast.10, s32[32,512]{1,0:T(8,128)} %bitcast.7), custom_call_target="tpu_custom_call" | custom-call | tf_op jit(solution)/shard_map/step/pallas_call | solution.py:387
  92.2 1.6 %copy.11 = f32[64,768]{1,0:T(8,128)} copy(f32[64,768]{1,0:T(8,128)} %get-tuple-element.4) | data formatting | bytes 393216
  93.8 2.7 %copy.12 = f32[512,768]{1,0:T(8,128)} copy(f32[512,768]{1,0:T(8,128)} %get-tuple-element.5) | data formatting | bytes 3145728

commit v2 on v0

v2 whole, which is shorter than its diff:
```python
import functools
import heapq
import math

import jax
import jax.numpy as jnp
from jax import lax
from jax.experimental import pallas as pl
from jax.experimental.pallas import tpu as pltpu
from jax.sharding import PartitionSpec as P

MESH = pl.DeviceIdType.MESH
NT = (((1,), (1,)), ((), ()))
TN = (((0,), (0,)), ((), ()))


def rem4(v):
    return lax.rem(v + 8, 4)


class Place:
    def __init__(self):
        self.e = lax.axis_index("enc")
        lab = lax.axis_index("lab")
        self.c = lax.rem(lab, 2)
        self.x = lax.rem(lax.div(lab, 2), 4)
        self.y = lax.rem(lax.div(lab, 8), 4)
        self.h = lax.div(lab, 32)

    def lab_of(self, h, y, x, c):
        return ((h * 4 + y) * 4 + x) * 2 + c

    def along_x(self, k):
        return (self.e, self.lab_of(self.h, self.y, rem4(self.x + k), self.c))

    def along_y(self, k):
        return (self.e, self.lab_of(self.h, rem4(self.y + k), self.x, self.c))

    def sibling(self):
        return (self.e, self.lab_of(self.h, self.y, self.x, 1 - self.c))

    def mirror(self):
        return (3 - self.e, self.lab_of(1 - self.h, self.y, self.x, self.c))

    def across(self, k):
        return (rem4(self.e + k), self.lab_of(1 - self.h, self.y, self.x, self.c))

    def along_enc(self, k):
        return (rem4(self.e + k), self.lab_of(self.h, self.y, self.x, self.c))


class Copy:
    def __init__(self, mail, n, src, dst, device):
        self.mail, self.n, self.src, self.dst, self.device = mail, n, src, dst, device

    def made(self):
        return pltpu.make_async_remote_copy(
            src_ref=self.src[0].at[self.src[1:]],
            dst_ref=self.dst[0].at[self.dst[1:]],
            send_sem=self.mail.send.at[self.n],
            recv_sem=self.mail.recv.at[self.n],
            device_id=self.device,
            device_id_type=MESH,
        )

    def wait_recv(self):
        self.made().wait_recv()


class Mail:
    def __init__(self, send, recv):
        self.send, self.recv, self.sent = send, recv, []

    def post(self, src, dst, device):
        copy = Copy(self, len(self.sent), src, dst, device)
        copy.made().start()
        self.sent.append(copy)
        return copy

    def finish(self):
        for copy in self.sent:
            copy.made().wait_send()


RIGHT, LEFT, UP, DOWN = range(4)


def onward(key):
    rh, k, s, ry, rx = key
    first, second = (rx, ry) if k == 0 else (ry, rx)
    ways = ((RIGHT, LEFT), (UP, DOWN)) if k == 0 else ((UP, DOWN), (RIGHT, LEFT))

    def there(f, t):
        return (rh, k, s, t, f) if k == 0 else (rh, k, s, f, t)

    out = []
    if second == 0:
        if first == 0:
            out += [(ways[0][0], there(3, 0)), (ways[0][1], there(1, 0))]
        if first == (1 if s else 3):
            out += [(ways[0][s], there(2, 0))]
        out += [(ways[1][0], there(first, 3)), (ways[1][1], there(first, 1))]
    if second == (1 if s else 3):
        out += [(ways[1][s], there(first, 2))]
    return out


def gather_plan(chunks, wire=0.55, hop=2.0, chunk_time=1.9):
    plan, events, free, now = [], [], [0.0] * 4, 0.0
    parts = [(k, s) for s in (0, 1) for k in (0, 1)]
    for n, (k, s) in enumerate(parts):
        heapq.heappush(events, (0.0, n, (0, k, s, 0, 0)))
        heapq.heappush(events, (4.0 + 1.05 * n, 4 + n, (1, k, s, 0, 0)))
    order, have = 8, set()
    todo = list(chunks)

    def runnable():
        for rh, k, pair in todo:
            firsts, seconds = (2 * pair, 2 * pair + 1), range(4)
            places = [(t, f) if k == 0 else (f, t) for f in firsts for t in seconds]
            if all((rh, k, s) + place in have for place in places for s in (0, 1)):
                return rh, k, pair
        return None

    while events or todo:
        chunk = runnable()
        quiet = not events or events[0][0] > now + 0.5 or min(free) > now + 1.5
        if chunk and quiet:
            todo.remove(chunk)
            plan.append(("chunk",) + chunk)
            now += chunk_time
            continue
        time, _, key = heapq.heappop(events)
        now = max(now, time) + 0.03
        plan.append(("wait", key))
        for way, then in onward(key):
            free[way] = max(now, free[way]) + wire
            heapq.heappush(events, (free[way] + hop, order, then))
            order += 1
            now += 0.03
            plan.append(("send", key, then, way))
        have.add(key)
    return plan


class RingSum:
    def __init__(self, mail, out, into, rh, groups, value, plus, minus):
        self.mail, self.out, self.into, self.rh, self.groups, self.value = mail, out, into, rh, groups, value
        self.plus, self.minus = plus, minus
        self.copies = {}

    def fill(self, way, slot, make):
        def one(g, carry):
            self.out[self.rh, way, slot, g] = make(g).astype(jnp.bfloat16)
            return carry

        lax.fori_loop(0, self.groups, one, 0, unroll=True)
        self.copies[way, slot] = self.mail.post(
            (self.out, self.rh, way, slot), (self.into, self.rh, way, slot), self.minus if way else self.plus
        )

    def far(self):
        self.fill(0, 0, lambda g: self.value(g, 2, 0))
        self.fill(1, 0, lambda g: self.value(g, 2, 1))

    def near(self, way):
        self.fill(way, 1, lambda g: self.value(g, 3 if way else 1, 0 if way else 1))

    def got(self, way, slot, g):
        return self.into[self.rh, way, slot, g].astype(jnp.float32)

    def relay(self, way):
        self.copies[way, 0].wait_recv()
        self.fill(way, 2, lambda g: self.value(g, 3 if way else 1, way) + self.got(way, 0, g))

    def collect(self, store):
        for way in (0, 1):
            for slot in (1, 2):
                self.copies[way, slot].wait_recv()

        def one(g, carry):
            store(g, 0, self.value(g, 0, 0) + self.got(0, 2, g) + self.got(1, 1, g))
            store(g, 1, self.value(g, 0, 1) + self.got(0, 1, g) + self.got(1, 2, g))
            return carry

        lax.fori_loop(0, self.groups, one, 0, unroll=True)


def slot_weights(live_ref, pos_ref, neg_ref, sw, side, panel, slots, nneg):
    docs = pos_ref.shape[1]
    label = lax.broadcasted_iota(jnp.int32, (panel, docs), 0)
    for s in range(slots):
        hot = jnp.where(pos_ref[pl.ds(s, 1), :] == label, 1.0, 0.0)
        count = hot
        for k in range(nneg):
            count += jnp.where(neg_ref[pl.ds(s * nneg + k, 1), :] == label, 1.0, 0.0)
        half = 0.5 * live_ref[pl.ds(s, 1), :].astype(jnp.float32)
        sw[side, s] = half * count * (1.0 - 2.0 * hot)


def kernel(
    scale, panel, slots, nneg,
    emb_ref, cls_ref, valid_ref, short_ref, live_ref, pos_ref, neg_ref,
    wg_ref, eg_ref,
    G, emb2, embh, sw, dl, K, eg, eg_in, short_in, live_in, pos_in, neg_in,
    a1_out, a1_in, b1_out, b1_in, sum_a, sum_b, a2_out, a2_in, b2_out, b2_in,
    V, z_out, z_in, part,
    send, recv,
):
    at = Place()
    docs, width = emb_ref.shape
    right, left, up, down = at.along_x(1), at.along_x(-1), at.along_y(1), at.along_y(-1)
    sibling = at.sibling()
    barrier = pltpu.get_barrier_semaphore()
    partners = [right, left, up, down, sibling]
    partners += [at.along_enc(k) for k in range(1, 4)] + [at.across(k) for k in range(4)]
    for device in partners:
        pl.semaphore_signal(barrier, inc=1, device_id=device, device_id_type=MESH)

    rows = lax.broadcasted_iota(jnp.int32, (panel, panel), 0)
    cols = lax.broadcasted_iota(jnp.int32, (panel, panel), 1)
    flags = jnp.where(rows == cols, valid_ref[...].astype(jnp.float32), 0.0)
    valid = jnp.sum(flags, axis=1, keepdims=True)
    mine = (cls_ref[...] * valid).astype(jnp.bfloat16)
    G[0, 0, 0] = mine.reshape(2, 2, 16, width)
    pl.semaphore_wait(barrier, len(partners))

    mail = Mail(send, recv)

    def score(rh, parts):
        blocks = []
        for k, pair in parts:
            rows = pl.ds(2 * pair, 2)
            block = G[rh, :, rows, 0] if k == 0 else G[rh, rows, :, 1]
            blocks.append(block.reshape(4 * panel, width))
        w = blocks[0] if len(blocks) == 1 else jnp.concatenate(blocks, axis=0)
        labels = w.shape[0]
        half_logits = lax.dot_general(w, embh[...], NT, preferred_element_type=jnp.float32)
        h = at.h if rh == 0 else 1 - at.h
        row = 0
        for k, pair in parts:
            for a in range(8):
                ry, rx = (a // 2, 2 * pair + a % 2) if k == 0 else (2 * pair + a // 4, a % 4)
                cluster = at.lab_of(h, rem4(at.y + ry), rem4(at.x + rx), at.c)
                for side, short in enumerate((short_ref, short_in)):
                    hw = None
                    for s in range(slots):
                        term = sw[side, s, pl.ds(k * panel // 2, panel // 2)] * jnp.where(
                            short[pl.ds(s, 1), :] == cluster, 1.0, 0.0
                        )
                        hw = term if hw is None else hw + term
                    t = jnp.tanh(half_logits[row : row + panel // 2, side * docs : (side + 1) * docs])
                    dl[pl.ds(row, panel // 2), pl.ds(side * docs, docs)] = (jnp.abs(hw) * t + hw).astype(jnp.bfloat16)
                row += panel // 2
        d = dl[pl.ds(0, labels), :]
        grad = jnp.dot(d, emb2[...], preferred_element_type=jnp.float32)
        for n, (k, pair) in enumerate(parts):
            rows = pl.ds(2 * pair, 2)
            part_grad = grad[n * 4 * panel : (n + 1) * 4 * panel]
            if k == 0:
                K[rh, :, rows, 0] = part_grad.reshape(4, 2, 2, 16, width)
            else:
                K[rh, rows, :, 1] = part_grad.reshape(2, 4, 2, 16, width)
        eg[...] += lax.dot_general(d, w, TN, preferred_element_type=jnp.float32)

    def term_a(rh):
        return lambda g, rel, s: K[rh, g, rel, 0, s]

    def term_b(rh):
        return lambda g, rel, s: K[rh, rel, g, 1, s]

    def ring(out, into, rh, groups, value, plus, minus):
        return RingSum(mail, out, into, rh, groups, value, plus, minus)

    a1 = [ring(a1_out, a1_in, rh, 4, term_a(rh), right, left) for rh in (0, 1)]
    b1 = [ring(b1_out, b1_in, rh, 4, term_b(rh), up, down) for rh in (0, 1)]
    a2 = [ring(a2_out, a2_in, rh, 1, lambda g, rel, s, rh=rh: sum_a[rh, rel, s], up, down) for rh in (0, 1)]
    b2 = [ring(b2_out, b2_in, rh, 1, lambda g, rel, s, rh=rh: sum_b[rh, rel, s], right, left) for rh in (0, 1)]

    def first_relays(rh, way):
        a1[rh].relay(way)
        b1[rh].relay(way)

    def first_far(rh):
        a1[rh].far()
        b1[rh].far()
        a1[rh].near(1)
        b1[rh].near(1)

    def first_near(rh):
        a1[rh].near(0)
        b1[rh].near(0)

    def second_sends(rh):
        def store_a(g, s, v):
            sum_a[rh, g, s] = v

        def store_b(g, s, v):
            sum_b[rh, g, s] = v

        a1[rh].collect(store_a)
        a2[rh].far()
        b1[rh].collect(store_b)
        b2[rh].far()
        for way in (0, 1):
            a2[rh].near(way)
            b2[rh].near(way)

    def second_relays(rh):
        for way in (0, 1):
            a2[rh].relay(way)
            b2[rh].relay(way)

    def plane_sum(rh):
        def store(half):
            def put(g, s, v):
                V[rh, 2 * half + s] = v
                z_out[rh, 2 * half + s] = v.astype(jnp.bfloat16)

            return put

        a2[rh].collect(store(0))
        b2[rh].collect(store(1))

    slices = []

    def z_sends(rh):
        for k in range(1 - rh, 4):
            device = at.across(k) if rh else at.along_enc(k)
            slices.append(mail.post((z_out, rh, rem4(at.e + k)), (z_in, len(slices)), device))

    posted = {}
    devices = (right, left, up, down)
    mirror = at.mirror()
    parts = [(k, s) for s in (0, 1) for k in (0, 1)]

    def piece(key):
        rh, k, s, ry, rx = key
        return (G, rh, ry, rx, k, s)

    def follow(plan):
        for what in plan:
            if what[0] == "chunk":
                score(what[1], [what[2:]])
            elif what[0] == "send":
                posted[what[2]] = mail.post(piece(what[1]), piece(what[2]), devices[what[3]])
            elif what[1] in posted:
                posted[what[1]].wait_recv()

    plan = gather_plan([(0, k, pair) for pair in (1, 0) for k in (0, 1)])
    opening = next(n for n, what in enumerate(plan) if what[0] == "wait" and (what[1][0] or what[1][3] or what[1][4]))
    follow(plan[:opening])
    for k, s in parts:
        posted[1, k, s, 0, 0] = mail.post((G, 0, 0, 0, k, s), (G, 1, 0, 0, k, s), mirror)
    whole = slice(None)
    shared = [
        mail.post((src, whole), (dst, whole), sibling)
        for src, dst in ((short_ref, short_in), (live_ref, live_in), (pos_ref, pos_in), (neg_ref, neg_in))
    ]
    shared.append(mail.post((emb_ref, whole), (emb2, pl.ds(docs, docs)), sibling))
    emb2[pl.ds(0, docs), :] = emb_ref[...]
    embh[pl.ds(0, docs), :] = emb_ref[...] * jnp.bfloat16(0.5)
    slot_weights(live_ref, pos_ref, neg_ref, sw, 0, panel, slots, nneg)
    eg[...] = jnp.zeros_like(eg)
    for copy in shared:
        copy.wait_recv()
    slot_weights(live_in, pos_in, neg_in, sw, 1, panel, slots, nneg)
    embh[pl.ds(docs, docs), :] = emb2[pl.ds(docs, docs), :] * jnp.bfloat16(0.5)
    follow(plan[opening:])
    first_far(0)
    first_near(0)
    score(1, [(0, 1), (1, 1)])
    first_relays(0, 0)
    first_relays(0, 1)
    first_far(1)
    score(1, [(0, 0), (1, 0)])
    returned = mail.post((eg, pl.ds(docs, docs)), (eg_in, whole), sibling)
    first_near(1)
    first_relays(1, 1)
    first_relays(1, 0)
    second_sends(0)
    second_relays(0)
    second_sends(1)
    plane_sum(0)
    z_sends(0)
    returned.wait_recv()
    eg_ref[...] = eg[pl.ds(0, docs), :] + eg_in[...]
    second_relays(1)
    plane_sum(1)
    z_sends(1)

    total = V[0, at.e]
    for k, copy in enumerate(slices):
        copy.wait_recv()
        total += z_in[k].astype(jnp.float32)
    part[at.e] = total * scale
    shares = [mail.post((part, at.e), (part, at.e), at.along_enc(k)) for k in range(1, 4)]
    for copy in shares:
        copy.wait_recv()
    wg_ref[...] = part[...].reshape(panel, width) * valid

    mail.finish()


def shards(embeddings, classifier, label_valid, shortlist, slot_live, positive, negative):
    lab_count = lax.axis_size("lab")
    enc_count = lax.axis_size("enc")
    docs, width = embeddings.shape
    panel = classifier.shape[0]
    slots = shortlist.shape[1]
    nneg = negative.shape[2]
    scale = 1.0 / math.sqrt(docs * enc_count * slots)
    by_slot = lambda a: a.transpose(1, 0)
    vmem = pl.BlockSpec(memory_space=pltpu.VMEM)
    bf16, f32 = jnp.bfloat16, jnp.float32
    piece = (16, width)
    return pl.pallas_call(
        functools.partial(kernel, scale, panel, slots, nneg),
        out_shape=(
            jax.ShapeDtypeStruct((panel, width), f32),
            jax.ShapeDtypeStruct((docs, width), f32),
        ),
        in_specs=[vmem] * 7,
        out_specs=(vmem, vmem),
        scratch_shapes=[
            pltpu.VMEM((2, 4, 4, 2, 2) + piece, bf16),
            pltpu.VMEM((2 * docs, width), bf16),
            pltpu.VMEM((2 * docs, width), bf16),
            pltpu.VMEM((2, slots, panel, docs), f32),
            pltpu.VMEM((8 * panel, 2 * docs), bf16),
            pltpu.VMEM((2, 4, 4, 2, 2) + piece, f32),
            pltpu.VMEM((2 * docs, width), f32),
            pltpu.VMEM((docs, width), f32),
            pltpu.VMEM((slots, docs), jnp.int32),
            pltpu.VMEM((slots, docs), jnp.int32),
            pltpu.VMEM((slots, docs), jnp.int32),
            pltpu.VMEM((slots * nneg, docs), jnp.int32),
            pltpu.VMEM((2, 2, 3, 4) + piece, bf16),
            pltpu.VMEM((2, 2, 3, 4) + piece, bf16),
            pltpu.VMEM((2, 2, 3, 4) + piece, bf16),
            pltpu.VMEM((2, 2, 3, 4) + piece, bf16),
            pltpu.VMEM((2, 4, 2) + piece, f32),
            pltpu.VMEM((2, 4, 2) + piece, f32),
            pltpu.VMEM((2, 2, 3, 1) + piece, bf16),
            pltpu.VMEM((2, 2, 3, 1) + piece, bf16),
            pltpu.VMEM((2, 2, 3, 1) + piece, bf16),
            pltpu.VMEM((2, 2, 3, 1) + piece, bf16),
            pltpu.VMEM((2, 4) + piece, f32),
            pltpu.VMEM((2, 4) + piece, bf16),
            pltpu.VMEM((7,) + piece, bf16),
            pltpu.VMEM((4,) + piece, f32),
            pltpu.SemaphoreType.DMA((192,)),
            pltpu.SemaphoreType.DMA((192,)),
        ],
        compiler_params=pltpu.CompilerParams(
            collective_id=0, has_side_effects=True, vmem_limit_bytes=60 * 1024 * 1024
        ),
        name="step",
    )(
        embeddings,
        classifier,
        label_valid.reshape(1, panel),
        by_slot(shortlist),
        by_slot(slot_live),
        by_slot(positive),
        negative.transpose(1, 2, 0).reshape(slots * nneg, docs),
    )


def solution(mesh):
    in_specs = (
        P(("enc", "lab"), None),
        P("lab", None),
        P("lab"),
        P(("enc", "lab"), None),
        P(("enc", "lab"), None),
        P(("enc", "lab"), None),
        P(("enc", "lab"), None, None),
    )
    out_specs = (P("lab", None), P(("enc", "lab"), None))
    return jax.shard_map(shards, mesh=mesh, in_specs=in_specs, out_specs=out_specs, check_vma=False)
```

time: 588 us -> 81.6 us (0.14)
  waiting for transfers between devices: 255 us -> 0 us
  blocking collectives: 216 us -> 0 us
  Pallas kernels: 0 us -> 76.5 us
  matrix products: 47 us -> 0 us
  local copies, waits for them, and re-layouts: 46 us -> 4.27 us
  between operations: 14.5 us -> 0.64 us
  other arithmetic: 6.25 us -> 0 us
    reduce_scatter x1 -> x0, waiting for transfers between devices: 218 us -> none  [shards(): lax.psum_scatter(lax.dot_general(scored, embeddings, (((0,), (0,)), ((),...]
    unnamed x1 -> x0, blocking collectives: 216 us -> none
    pallas_call x0 -> x1, Pallas kernels: none -> 76.5 us  [shards(): pl.pallas_call(functools.partial(kernel, scale, panel, slots, nneg), out_...]
    dot_general x5 -> x0, matrix products: 47 us -> none  [the longest x1 11 us: absorb(): lax.dot_general(embeddings, w_piece, (((1,), (1,)), ((), ())), preferred_...]
    convert_element_type x4 -> x0, local copies, waits for them, and re-layouts: 43.5 us -> none  [the longest x2 21.8 us: absorb(): target = target_all.astype(jnp.float32)]
    psum x1 -> x0, waiting for transfers between devices: 36.7 us -> none  [shards(): w_grad = lax.psum(partial_grad, 'enc') * scale_factor]
  transfers between devices with their start and end apart: 3 -> 0, of which waited for: 2 -> 0; matrix products, arithmetic and copies ran while one was open for 13% -> 0% of each run, Pallas kernels for 0% -> 0%
where the time goes in v2:
time: 81.6 us; the launch traced here: 81.4 us
  Pallas kernels  76.5 us (94%)
  local copies, waits for them, and re-layouts  4.27 us (5%)
    pallas_call x1, Pallas kernels, shards(): pl.pallas_call(functools.partial(kernel, scale, panel, slots, nneg), out_...  76.5 us
    unnamed x2, local copies, waits for them, and re-layouts  4.27 us

profile of v2, /device:TPU:32, one launch (start us, length us, event | category | flops | bytes accessed | tf_op | source)
XLA Modules:
  0.0 81.4 jit_solution(1025636417046379367)
XLA Ops:
  0.6 76.5 %step.1 = (f32[64,768]{1,0:T(8,128)}, f32[512,768]{1,0:T(8,128)}) custom-call(bf16[512,768]{1,0:T(8,128)(2,1)} %emb_ref.1, f32[64,768]{1,0:T(8,128)} %cls_ref.1, s32[1,64]{1,0:T(1,128)} %bitcast.11, s32[4,512]{1,0:T(4,128)} %bitcast.8, s32[4,512]{1,0:T(4,128)} %bitcast.9, s32[4,512]{1,0:T(4,128)} %bitcast.10, s32[32,512]{1,0:T(8,128)} %bitcast.7), custom_call_target="tpu_custom_call" | custom-call | tf_op jit(solution)/shard_map/step/pallas_call | solution.py:417
  77.1 1.6 %copy.11 = f32[64,768]{1,0:T(8,128)} copy(f32[64,768]{1,0:T(8,128)} %get-tuple-element.4) | data formatting | bytes 393216
  78.7 2.7 %copy.12 = f32[512,768]{1,0:T(8,128)} copy(f32[512,768]{1,0:T(8,128)} %get-tuple-element.5) | data formatting | bytes 3145728

commit v3 on v2

--- a/solution.py
+++ b/solution.py
@@ -90,36 +90,34 @@
     first, second = (rx, ry) if k == 0 else (ry, rx)
     ways = ((RIGHT, LEFT), (UP, DOWN)) if k == 0 else ((UP, DOWN), (RIGHT, LEFT))
 
-    def there(f, t):
+    def there(s, f, t):
         return (rh, k, s, t, f) if k == 0 else (rh, k, s, f, t)
 
     out = []
     if second == 0:
         if first == 0:
-            out += [(ways[0][0], there(3, 0)), (ways[0][1], there(1, 0))]
-        if first == (1 if s else 3):
-            out += [(ways[0][s], there(2, 0))]
-        out += [(ways[1][0], there(first, 3)), (ways[1][1], there(first, 1))]
-    if second == (1 if s else 3):
-        out += [(ways[1][s], there(first, 2))]
+            out += [(ways[0][0], there(None, 3, 0), 4), (ways[0][1], there(None, 1, 0), 4)]
+        elif first != 2:
+            s = 0 if first == 3 else 1
+            out += [(ways[0][s], there(s, 2, 0), 3)]
+        out += [(ways[1][0], there(None, first, 3), 2), (ways[1][1], there(None, first, 1), 2)]
+    elif second != 2:
+        s = 0 if second == 3 else 1
+        out += [(ways[1][s], there(s, first, 2), 1)]
     return out
 
 
-def gather_plan(chunks, wire=0.55, hop=2.0, chunk_time=1.9):
-    plan, events, free, now = [], [], [0.0] * 4, 0.0
-    parts = [(k, s) for s in (0, 1) for k in (0, 1)]
-    for n, (k, s) in enumerate(parts):
-        heapq.heappush(events, (0.0, n, (0, k, s, 0, 0)))
-        heapq.heappush(events, (4.0 + 1.05 * n, 4 + n, (1, k, s, 0, 0)))
-    order, have = 8, set()
-    todo = list(chunks)
+def gather_plan(chunks, wire=0.6, hop=2.6, chunk_time=1.9):
+    plan, free, now = [], [0.0] * 4, 0.0
+    events = [(0.0, k, (0, k, None, 0, 0)) for k in (0, 1)] + [(5.0 + 2.0 * k, 2 + k, (1, k, None, 0, 0)) for k in (0, 1)]
+    heapq.heapify(events)
+    order, have, todo = 4, set(), list(chunks)
 
     def runnable():
-        for rh, k, pair in todo:
-            firsts, seconds = (2 * pair, 2 * pair + 1), range(4)
-            places = [(t, f) if k == 0 else (f, t) for f in firsts for t in seconds]
-            if all((rh, k, s) + place in have for place in places for s in (0, 1)):
-                return rh, k, pair
+        for rh, parts in todo:
+            places = [(k, t, f) if k == 0 else (k, f, t) for k, f in parts for t in range(4)]
+            if all((rh,) + place in have for place in places):
+                return rh, parts
         return None
 
     while events or todo:
@@ -130,16 +128,26 @@
             plan.append(("chunk",) + chunk)
             now += chunk_time
             continue
-        time, _, key = heapq.heappop(events)
-        now = max(now, time) + 0.03
-        plan.append(("wait", key))
-        for way, then in onward(key):
-            free[way] = max(now, free[way]) + wire
+        now = max(now, events[0][0])
+        sends = []
+        while events and events[0][0] <= now:
+            key = heapq.heappop(events)[2]
+            plan.append(("wait", key))
+            now += 0.03
+            rh, k, s, ry, rx = key
+            if s is not None:
+                if (rh, k, 1 - s, ry, rx) not in have:
+                    have.add(key)
+                    continue
+                key = (rh, k, None, ry, rx)
+            have.add((rh, k, ry, rx))
+            sends += [(-left, rh, way, key, then) for way, then, left in onward(key)]
+        for _, _, way, key, then in sorted(sends, key=lambda send: send[:3]):
+            free[way] = max(now, free[way]) + (wire if then[2] is not None else 2 * wire)
             heapq.heappush(events, (free[way] + hop, order, then))
             order += 1
             now += 0.03
             plan.append(("send", key, then, way))
-        have.add(key)
     return plan
 
 
@@ -228,19 +236,15 @@
     mail = Mail(send, recv)
 
     def score(rh, parts):
-        blocks = []
-        for k, pair in parts:
-            rows = pl.ds(2 * pair, 2)
-            block = G[rh, :, rows, 0] if k == 0 else G[rh, rows, :, 1]
-            blocks.append(block.reshape(4 * panel, width))
-        w = blocks[0] if len(blocks) == 1 else jnp.concatenate(blocks, axis=0)
+        w = [G[rh, :, f, 0] if k == 0 else G[rh, f, :, 1] for k, f in parts]
+        w = jnp.concatenate([block.reshape(2 * panel, width) for block in w], axis=0)
         labels = w.shape[0]
         half_logits = lax.dot_general(w, embh[...], NT, preferred_element_type=jnp.float32)
         h = at.h if rh == 0 else 1 - at.h
         row = 0
-        for k, pair in parts:
-            for a in range(8):
-                ry, rx = (a // 2, 2 * pair + a % 2) if k == 0 else (2 * pair + a // 4, a % 4)
+        for k, f in parts:
+            for t in range(4):
+                ry, rx = (t, f) if k == 0 else (f, t)
                 cluster = at.lab_of(h, rem4(at.y + ry), rem4(at.x + rx), at.c)
                 for side, short in enumerate((short_ref, short_in)):
                     hw = None
@@ -254,13 +258,12 @@
                 row += panel // 2
         d = dl[pl.ds(0, labels), :]
         grad = jnp.dot(d, emb2[...], preferred_element_type=jnp.float32)
-        for n, (k, pair) in enumerate(parts):
-            rows = pl.ds(2 * pair, 2)
-            part_grad = grad[n * 4 * panel : (n + 1) * 4 * panel]
+        for n, (k, f) in enumerate(parts):
+            part_grad = grad[n * 2 * panel : (n + 1) * 2 * panel].reshape(4, 2, 16, width)
             if k == 0:
-                K[rh, :, rows, 0] = part_grad.reshape(4, 2, 2, 16, width)
+                K[rh, :, f, 0] = part_grad
             else:
-                K[rh, rows, :, 1] = part_grad.reshape(2, 4, 2, 16, width)
+                K[rh, f, :, 1] = part_grad
         eg[...] += lax.dot_general(d, w, TN, preferred_element_type=jnp.float32)
 
     def term_a(rh):
@@ -277,19 +280,19 @@
     a2 = [ring(a2_out, a2_in, rh, 1, lambda g, rel, s, rh=rh: sum_a[rh, rel, s], up, down) for rh in (0, 1)]
     b2 = [ring(b2_out, b2_in, rh, 1, lambda g, rel, s, rh=rh: sum_b[rh, rel, s], right, left) for rh in (0, 1)]
 
-    def first_relays(rh, way):
-        a1[rh].relay(way)
-        b1[rh].relay(way)
-
     def first_far(rh):
         a1[rh].far()
         b1[rh].far()
-        a1[rh].near(1)
-        b1[rh].near(1)
 
     def first_near(rh):
-        a1[rh].near(0)
-        b1[rh].near(0)
+        for way in (0, 1):
+            a1[rh].near(way)
+            b1[rh].near(way)
+
+    def first_relays(rh):
+        for way in (0, 1):
+            a1[rh].relay(way)
+            b1[rh].relay(way)
 
     def second_sends(rh):
         def store_a(g, s, v):
@@ -332,26 +335,26 @@
     posted = {}
     devices = (right, left, up, down)
     mirror = at.mirror()
-    parts = [(k, s) for s in (0, 1) for k in (0, 1)]
 
     def piece(key):
         rh, k, s, ry, rx = key
-        return (G, rh, ry, rx, k, s)
+        return (G, rh, ry, rx, k) if s is None else (G, rh, ry, rx, k, s)
 
     def follow(plan):
         for what in plan:
             if what[0] == "chunk":
-                score(what[1], [what[2:]])
+                score(*what[1:])
             elif what[0] == "send":
-                posted[what[2]] = mail.post(piece(what[1]), piece(what[2]), devices[what[3]])
+                src = what[1] if what[2][2] is None else what[1][:2] + what[2][2:3] + what[1][3:]
+                posted[what[2]] = mail.post(piece(src), piece(what[2]), devices[what[3]])
             elif what[1] in posted:
                 posted[what[1]].wait_recv()
 
-    plan = gather_plan([(0, k, pair) for pair in (1, 0) for k in (0, 1)])
+    plan = gather_plan([(0, ((k, f), (k, f + 1))) for f in (2, 0) for k in (0, 1)])
     opening = next(n for n, what in enumerate(plan) if what[0] == "wait" and (what[1][0] or what[1][3] or what[1][4]))
     follow(plan[:opening])
-    for k, s in parts:
-        posted[1, k, s, 0, 0] = mail.post((G, 0, 0, 0, k, s), (G, 1, 0, 0, k, s), mirror)
+    for k in (0, 1):
+        posted[1, k, None, 0, 0] = mail.post((G, 0, 0, 0, k), (G, 1, 0, 0, k), mirror)
     whole = slice(None)
     shared = [
         mail.post((src, whole), (dst, whole), sibling)
@@ -369,15 +372,14 @@
     follow(plan[opening:])
     first_far(0)
     first_near(0)
-    score(1, [(0, 1), (1, 1)])
-    first_relays(0, 0)
-    first_relays(0, 1)
+    score(1, ((0, 2), (1, 2)))
+    first_relays(0)
     first_far(1)
-    score(1, [(0, 0), (1, 0)])
+    score(1, ((0, 1), (0, 3), (1, 1), (1, 3)))
+    first_near(1)
+    first_relays(1)
+    score(1, ((0, 0), (1, 0)))
     returned = mail.post((eg, pl.ds(docs, docs)), (eg_in, whole), sibling)
-    first_near(1)
-    first_relays(1, 1)
-    first_relays(1, 0)
     second_sends(0)
     second_relays(0)
     second_sends(1)
@@ -416,10 +418,7 @@
     piece = (16, width)
     return pl.pallas_call(
         functools.partial(kernel, scale, panel, slots, nneg),
-        out_shape=(
-            jax.ShapeDtypeStruct((panel, width), f32),
-            jax.ShapeDtypeStruct((docs, width), f32),
-        ),
+        out_shape=(pltpu.VMEM((panel, width), f32), pltpu.VMEM((docs, width), f32)),
         in_specs=[vmem] * 7,
         out_specs=(vmem, vmem),
         scratch_shapes=[

time: 81.6 us -> 75.8 us (0.929)
  Pallas kernels: 76.5 us -> 73 us
  local copies, waits for them, and re-layouts: 4.27 us -> 1.82 us
    pallas_call x1, Pallas kernels: 76.5 us -> 73 us  [shards(): pl.pallas_call(functools.partial(kernel, scale, panel, slots, nneg), out_...]
    unnamed x2, local copies, waits for them, and re-layouts: 4.27 us -> 1.82 us
where the time goes in v3:
time: 75.8 us; the launch traced here: 75.5 us
  Pallas kernels  73 us (96%)
  local copies, waits for them, and re-layouts  1.82 us (2%)
    pallas_call x1, Pallas kernels, shards(): pl.pallas_call(functools.partial(kernel, scale, panel, slots, nneg), out_...  73 us
    unnamed x2, local copies, waits for them, and re-layouts  1.82 us

profile of v3, /device:TPU:32, one launch (start us, length us, event | category | flops | bytes accessed | tf_op | source)
XLA Modules:
  0.0 75.5 jit_solution(10494385520220025274)
XLA Ops:
  0.6 73.0 %step.1 = (f32[64,768]{1,0:T(8,128)S(1)}, f32[512,768]{1,0:T(8,128)S(1)}) custom-call(bf16[512,768]{1,0:T(8,128)(2,1)} %emb_ref.1, f32[64,768]{1,0:T(8,128)} %cls_ref.1, s32[1,64]{1,0:T(1,128)} %bitcast.11, s32[4,512]{1,0:T(4,128)} %bitcast.8, s32[4,512]{1,0:T(4,128)} %bitcast.9, s32[4,512]{1,0:T(4,128)} %bitcast.10, s32[32,512]{1,0:T(8,128)} %bitcast.7), custom_call_target="tpu_custom_call" | custom-call | tf_op jit(solution)/shard_map/step/pallas_call | solution.py:419
  73.7 0.7 copy.11
  74.4 1.1 %copy.12 = f32[512,768]{1,0:T(8,128)} copy(f32[512,768]{1,0:T(8,128)S(1)} %get-tuple-element.3) | data formatting | bytes 3145728

commit v4 on v3

--- a/solution.py
+++ b/solution.py
@@ -107,11 +107,11 @@
     return out
 
 
-def gather_plan(chunks, wire=0.6, hop=2.6, chunk_time=1.9):
+def gather_plan(chunks, rings, wire=0.6, hop=2.6, chunk_time=0.95):
     plan, free, now = [], [0.0] * 4, 0.0
     events = [(0.0, k, (0, k, None, 0, 0)) for k in (0, 1)] + [(5.0 + 2.0 * k, 2 + k, (1, k, None, 0, 0)) for k in (0, 1)]
     heapq.heapify(events)
-    order, have, todo = 4, set(), list(chunks)
+    order, have, todo, rings = 4, set(), list(chunks), list(rings)
 
     def runnable():
         for rh, parts in todo:
@@ -126,7 +126,17 @@
         if chunk and quiet:
             todo.remove(chunk)
             plan.append(("chunk",) + chunk)
-            now += chunk_time
+            now += chunk_time * len(chunk[1])
+            continue
+        for ring in list(rings):
+            needs, way, message = ring
+            if not any(rest in needs for rest in todo) and free[way] < now + 0.3:
+                rings.remove(ring)
+                plan.append(("ring",) + message)
+                free[way] = max(now, free[way]) + 8 * wire / 2
+                now += 0.1
+        if not events:
+            now += 0.5
             continue
         now = max(now, events[0][0])
         sends = []
@@ -148,7 +158,7 @@
             order += 1
             now += 0.03
             plan.append(("send", key, then, way))
-    return plan
+    return plan + [("ring",) + message for _, _, message in rings]
 
 
 class RingSum:
@@ -167,9 +177,8 @@
             (self.out, self.rh, way, slot), (self.into, self.rh, way, slot), self.minus if way else self.plus
         )
 
-    def far(self):
-        self.fill(0, 0, lambda g: self.value(g, 2, 0))
-        self.fill(1, 0, lambda g: self.value(g, 2, 1))
+    def far(self, way):
+        self.fill(way, 0, lambda g: self.value(g, 2, way))
 
     def near(self, way):
         self.fill(way, 1, lambda g: self.value(g, 3 if way else 1, 0 if way else 1))
@@ -208,15 +217,15 @@
 
 def kernel(
     scale, panel, slots, nneg,
-    emb_ref, cls_ref, valid_ref, short_ref, live_ref, pos_ref, neg_ref,
+    emb_hbm, cls_ref, valid_ref, short_hbm, live_hbm, pos_hbm, neg_hbm,
     wg_ref, eg_ref,
-    G, emb2, embh, sw, dl, K, eg, eg_in, short_in, live_in, pos_in, neg_in,
+    G, emb2, embh, sw, dl, K, eg, eg_in, short_ref, live_ref, pos_ref, neg_ref, short_in, live_in, pos_in, neg_in,
     a1_out, a1_in, b1_out, b1_in, sum_a, sum_b, a2_out, a2_in, b2_out, b2_in,
     V, z_out, z_in, part,
-    send, recv,
+    send, recv, fetch,
 ):
     at = Place()
-    docs, width = emb_ref.shape
+    docs, width = emb_hbm.shape
     right, left, up, down = at.along_x(1), at.along_x(-1), at.along_y(1), at.along_y(-1)
     sibling = at.sibling()
     barrier = pltpu.get_barrier_semaphore()
@@ -224,6 +233,22 @@
     partners += [at.along_enc(k) for k in range(1, 4)] + [at.across(k) for k in range(4)]
     for device in partners:
         pl.semaphore_signal(barrier, inc=1, device_id=device, device_id_type=MESH)
+
+    emb_ref = emb2.at[pl.ds(0, docs)]
+    fetched = [
+        pltpu.make_async_copy(src, dst, fetch.at[n])
+        for n, (src, dst) in enumerate(
+            (
+                (short_hbm, short_ref),
+                (live_hbm, live_ref),
+                (pos_hbm, pos_ref),
+                (neg_hbm, neg_ref),
+                (emb_hbm, emb_ref),
+            )
+        )
+    ]
+    for copy in fetched:
+        copy.start()
 
     rows = lax.broadcasted_iota(jnp.int32, (panel, panel), 0)
     cols = lax.broadcasted_iota(jnp.int32, (panel, panel), 1)
@@ -281,13 +306,9 @@
     b2 = [ring(b2_out, b2_in, rh, 1, lambda g, rel, s, rh=rh: sum_b[rh, rel, s], right, left) for rh in (0, 1)]
 
     def first_far(rh):
-        a1[rh].far()
-        b1[rh].far()
-
-    def first_near(rh):
-        for way in (0, 1):
-            a1[rh].near(way)
-            b1[rh].near(way)
+        for way in (0, 1):
+            a1[rh].far(way)
+            b1[rh].far(way)
 
     def first_relays(rh):
         for way in (0, 1):
@@ -302,9 +323,11 @@
             sum_b[rh, g, s] = v
 
         a1[rh].collect(store_a)
-        a2[rh].far()
+        for way in (0, 1):
+            a2[rh].far(way)
         b1[rh].collect(store_b)
-        b2[rh].far()
+        for way in (0, 1):
+            b2[rh].far(way)
         for way in (0, 1):
             a2[rh].near(way)
             b2[rh].near(way)
@@ -344,25 +367,37 @@
         for what in plan:
             if what[0] == "chunk":
                 score(*what[1:])
+            elif what[0] == "ring":
+                rh, of_b, distance, way = what[1:]
+                ring = (b1 if of_b else a1)[rh]
+                if distance == 2:
+                    ring.far(way)
+                else:
+                    ring.near(way)
             elif what[0] == "send":
                 src = what[1] if what[2][2] is None else what[1][:2] + what[2][2:3] + what[1][3:]
                 posted[what[2]] = mail.post(piece(src), piece(what[2]), devices[what[3]])
             elif what[1] in posted:
                 posted[what[1]].wait_recv()
 
-    plan = gather_plan([(0, ((k, f), (k, f + 1))) for f in (2, 0) for k in (0, 1)])
+    first_half = [(0, ((k, f), (k, f + 1))) for f in (2, 0) for k in (0, 1)]
+    own_place, beside = (1, ((0, 0), (1, 0))), (1, ((0, 1), (0, 3), (1, 1), (1, 3)))
+    rings = [(first_half, 2 * b + way, (0, b, d, way)) for d in (2, 1) for b in (0, 1) for way in (0, 1)]
+    rings += [([beside], 2 * b + way, (1, b, 1, way)) for b in (0, 1) for way in (0, 1)]
+    plan = gather_plan(first_half + [own_place, beside], rings)
     opening = next(n for n, what in enumerate(plan) if what[0] == "wait" and (what[1][0] or what[1][3] or what[1][4]))
     follow(plan[:opening])
     for k in (0, 1):
         posted[1, k, None, 0, 0] = mail.post((G, 0, 0, 0, k), (G, 1, 0, 0, k), mirror)
     whole = slice(None)
+    for copy in fetched:
+        copy.wait()
     shared = [
         mail.post((src, whole), (dst, whole), sibling)
         for src, dst in ((short_ref, short_in), (live_ref, live_in), (pos_ref, pos_in), (neg_ref, neg_in))
     ]
-    shared.append(mail.post((emb_ref, whole), (emb2, pl.ds(docs, docs)), sibling))
-    emb2[pl.ds(0, docs), :] = emb_ref[...]
-    embh[pl.ds(0, docs), :] = emb_ref[...] * jnp.bfloat16(0.5)
+    shared.append(mail.post((emb2, pl.ds(0, docs)), (emb2, pl.ds(docs, docs)), sibling))
+    embh[pl.ds(0, docs), :] = emb2[pl.ds(0, docs), :] * jnp.bfloat16(0.5)
     slot_weights(live_ref, pos_ref, neg_ref, sw, 0, panel, slots, nneg)
     eg[...] = jnp.zeros_like(eg)
     for copy in shared:
@@ -370,16 +405,11 @@
     slot_weights(live_in, pos_in, neg_in, sw, 1, panel, slots, nneg)
     embh[pl.ds(docs, docs), :] = emb2[pl.ds(docs, docs), :] * jnp.bfloat16(0.5)
     follow(plan[opening:])
-    first_far(0)
-    first_near(0)
     score(1, ((0, 2), (1, 2)))
+    first_far(1)
+    returned = mail.post((eg, pl.ds(docs, docs)), (eg_in, whole), sibling)
     first_relays(0)
-    first_far(1)
-    score(1, ((0, 1), (0, 3), (1, 1), (1, 3)))
-    first_near(1)
     first_relays(1)
-    score(1, ((0, 0), (1, 0)))
-    returned = mail.post((eg, pl.ds(docs, docs)), (eg_in, whole), sibling)
     second_sends(0)
     second_relays(0)
     second_sends(1)
@@ -413,13 +443,13 @@
     nneg = negative.shape[2]
     scale = 1.0 / math.sqrt(docs * enc_count * slots)
     by_slot = lambda a: a.transpose(1, 0)
-    vmem = pl.BlockSpec(memory_space=pltpu.VMEM)
+    vmem, hbm = pl.BlockSpec(memory_space=pltpu.VMEM), pl.BlockSpec(memory_space=pl.ANY)
     bf16, f32 = jnp.bfloat16, jnp.float32
     piece = (16, width)
     return pl.pallas_call(
         functools.partial(kernel, scale, panel, slots, nneg),
         out_shape=(pltpu.VMEM((panel, width), f32), pltpu.VMEM((docs, width), f32)),
-        in_specs=[vmem] * 7,
+        in_specs=[hbm, vmem, vmem] + [hbm] * 4,
         out_specs=(vmem, vmem),
         scratch_shapes=[
             pltpu.VMEM((2, 4, 4, 2, 2) + piece, bf16),
@@ -430,6 +460,10 @@
             pltpu.VMEM((2, 4, 4, 2, 2) + piece, f32),
             pltpu.VMEM((2 * docs, width), f32),
             pltpu.VMEM((docs, width), f32),
+            pltpu.VMEM((slots, docs), jnp.int32),
+            pltpu.VMEM((slots, docs), jnp.int32),
+            pltpu.VMEM((slots, docs), jnp.int32),
+            pltpu.VMEM((slots * nneg, docs), jnp.int32),
             pltpu.VMEM((slots, docs), jnp.int32),
             pltpu.VMEM((slots, docs), jnp.int32),
             pltpu.VMEM((slots, docs), jnp.int32),
@@ -450,6 +484,7 @@
             pltpu.VMEM((4,) + piece, f32),
             pltpu.SemaphoreType.DMA((192,)),
             pltpu.SemaphoreType.DMA((192,)),
+            pltpu.SemaphoreType.DMA((5,)),
         ],
         compiler_params=pltpu.CompilerParams(
             collective_id=0, has_side_effects=True, vmem_limit_bytes=60 * 1024 * 1024

time: 75.8 us -> 73.3 us (0.967)
  Pallas kernels: 73 us -> 70.7 us
    pallas_call x1, Pallas kernels: 73 us -> 70.7 us  [shards(): pl.pallas_call(functools.partial(kernel, scale, panel, slots, nneg), out_...]
where the time goes in v4:
time: 73.3 us; the launch traced here: 73.2 us
  Pallas kernels  70.7 us (96%)
  local copies, waits for them, and re-layouts  1.82 us (2%)
    pallas_call x1, Pallas kernels, shards(): pl.pallas_call(functools.partial(kernel, scale, panel, slots, nneg), out_...  70.7 us
    unnamed x2, local copies, waits for them, and re-layouts  1.82 us

profile of v4, /device:TPU:32, one launch (start us, length us, event | category | flops | bytes accessed | tf_op | source)
XLA Modules:
  0.0 73.2 jit_solution(7065688387668239926)
XLA Ops:
  0.6 70.7 %step.1 = (f32[64,768]{1,0:T(8,128)S(1)}, f32[512,768]{1,0:T(8,128)S(1)}) custom-call(bf16[512,768]{1,0:T(8,128)(2,1)} %emb_hbm.1, f32[64,768]{1,0:T(8,128)} %cls_ref.1, s32[1,64]{1,0:T(1,128)} %bitcast.11, s32[4,512]{1,0:T(4,128)} %bitcast.8, s32[4,512]{1,0:T(4,128)} %bitcast.9, s32[4,512]{1,0:T(4,128)} %bitcast.10, s32[32,512]{1,0:T(8,128)} %bitcast.7), custom_call_target="tpu_custom_call" | custom-call | tf_op jit(solution)/shard_map/step/pallas_call | solution.py:449
  71.4 0.7 copy.11
  72.0 1.1 %copy.12 = f32[512,768]{1,0:T(8,128)} copy(f32[512,768]{1,0:T(8,128)S(1)} %get-tuple-element.3) | data formatting | bytes 3145728

commit v5 on v4

--- a/solution.py
+++ b/solution.py
@@ -111,7 +111,7 @@
     plan, free, now = [], [0.0] * 4, 0.0
     events = [(0.0, k, (0, k, None, 0, 0)) for k in (0, 1)] + [(5.0 + 2.0 * k, 2 + k, (1, k, None, 0, 0)) for k in (0, 1)]
     heapq.heapify(events)
-    order, have, todo, rings = 4, set(), list(chunks), list(rings)
+    order, have, todo, rings, first_ring = 4, set(), list(chunks), list(rings), 1e9
 
     def runnable():
         for rh, parts in todo:
@@ -131,6 +131,9 @@
         for ring in list(rings):
             needs, way, message = ring
             if not any(rest in needs for rest in todo) and free[way] < now + 0.3:
+                if message[2] == 0 and now < first_ring + 5.5:
+                    continue
+                first_ring = min(first_ring, now)
                 rings.remove(ring)
                 plan.append(("ring",) + message)
                 free[way] = max(now, free[way]) + 8 * wire / 2
@@ -310,6 +313,11 @@
             a1[rh].far(way)
             b1[rh].far(way)
 
+    def first_near(rh):
+        for way in (0, 1):
+            a1[rh].near(way)
+            b1[rh].near(way)
+
     def first_relays(rh):
         for way in (0, 1):
             a1[rh].relay(way)
@@ -372,6 +380,8 @@
                 ring = (b1 if of_b else a1)[rh]
                 if distance == 2:
                     ring.far(way)
+                elif distance == 0:
+                    ring.relay(way)
                 else:
                     ring.near(way)
             elif what[0] == "send":
@@ -383,12 +393,12 @@
     first_half = [(0, ((k, f), (k, f + 1))) for f in (2, 0) for k in (0, 1)]
     own_place, beside = (1, ((0, 0), (1, 0))), (1, ((0, 1), (0, 3), (1, 1), (1, 3)))
     rings = [(first_half, 2 * b + way, (0, b, d, way)) for d in (2, 1) for b in (0, 1) for way in (0, 1)]
-    rings += [([beside], 2 * b + way, (1, b, 1, way)) for b in (0, 1) for way in (0, 1)]
+    rings += [(first_half + [own_place], 2 * b + way, (0, b, 0, way)) for b in (0, 1) for way in (0, 1)]
     plan = gather_plan(first_half + [own_place, beside], rings)
     opening = next(n for n, what in enumerate(plan) if what[0] == "wait" and (what[1][0] or what[1][3] or what[1][4]))
-    follow(plan[:opening])
     for k in (0, 1):
         posted[1, k, None, 0, 0] = mail.post((G, 0, 0, 0, k), (G, 1, 0, 0, k), mirror)
+    follow(plan[:opening])
     whole = slice(None)
     for copy in fetched:
         copy.wait()
@@ -400,24 +410,26 @@
     embh[pl.ds(0, docs), :] = emb2[pl.ds(0, docs), :] * jnp.bfloat16(0.5)
     slot_weights(live_ref, pos_ref, neg_ref, sw, 0, panel, slots, nneg)
     eg[...] = jnp.zeros_like(eg)
+    scoring = next(n for n, what in enumerate(plan) if what[0] == "chunk")
+    follow(plan[opening:scoring])
     for copy in shared:
         copy.wait_recv()
     slot_weights(live_in, pos_in, neg_in, sw, 1, panel, slots, nneg)
     embh[pl.ds(docs, docs), :] = emb2[pl.ds(docs, docs), :] * jnp.bfloat16(0.5)
-    follow(plan[opening:])
+    follow(plan[scoring:])
     score(1, ((0, 2), (1, 2)))
     first_far(1)
+    first_near(1)
     returned = mail.post((eg, pl.ds(docs, docs)), (eg_in, whole), sibling)
-    first_relays(0)
     first_relays(1)
     second_sends(0)
+    second_sends(1)
     second_relays(0)
-    second_sends(1)
-    plane_sum(0)
-    z_sends(0)
     returned.wait_recv()
     eg_ref[...] = eg[pl.ds(0, docs), :] + eg_in[...]
     second_relays(1)
+    plane_sum(0)
+    z_sends(0)
     plane_sum(1)
     z_sends(1)
 

time: 73.3 us -> 72.7 us (level)
  no operation moved by 1% of the time
where the time goes in v5:
time: 72.7 us; the launch traced here: 72.6 us
  Pallas kernels  70.1 us (96%)
  local copies, waits for them, and re-layouts  1.82 us (3%)
    pallas_call x1, Pallas kernels, shards(): pl.pallas_call(functools.partial(kernel, scale, panel, slots, nneg), out_...  70.1 us
    unnamed x2, local copies, waits for them, and re-layouts  1.82 us

profile of v5, /device:TPU:32, one launch (start us, length us, event | category | flops | bytes accessed | tf_op | source)
XLA Modules:
  0.0 72.6 jit_solution(1849912290870961445)
XLA Ops:
  0.6 70.1 %step.1 = (f32[64,768]{1,0:T(8,128)S(1)}, f32[512,768]{1,0:T(8,128)S(1)}) custom-call(bf16[512,768]{1,0:T(8,128)(2,1)} %emb_hbm.1, f32[64,768]{1,0:T(8,128)} %cls_ref.1, s32[1,64]{1,0:T(1,128)} %bitcast.11, s32[4,512]{1,0:T(4,128)} %bitcast.8, s32[4,512]{1,0:T(4,128)} %bitcast.9, s32[4,512]{1,0:T(4,128)} %bitcast.10, s32[32,512]{1,0:T(8,128)} %bitcast.7), custom_call_target="tpu_custom_call" | custom-call | tf_op jit(solution)/shard_map/step/pallas_call | solution.py:461
  70.8 0.7 copy.11
  71.4 1.1 %copy.12 = f32[512,768]{1,0:T(8,128)} copy(f32[512,768]{1,0:T(8,128)S(1)} %get-tuple-element.3) | data formatting | bytes 3145728

commit v6 on v5

--- a/solution.py
+++ b/solution.py
@@ -107,7 +107,7 @@
     return out
 
 
-def gather_plan(chunks, rings, wire=0.6, hop=2.6, chunk_time=0.95):
+def gather_plan(chunks, rings, wire=0.6, hop=3.2, chunk_time=0.95):
     plan, free, now = [], [0.0] * 4, 0.0
     events = [(0.0, k, (0, k, None, 0, 0)) for k in (0, 1)] + [(5.0 + 2.0 * k, 2 + k, (1, k, None, 0, 0)) for k in (0, 1)]
     heapq.heapify(events)
@@ -390,7 +390,7 @@
             elif what[1] in posted:
                 posted[what[1]].wait_recv()
 
-    first_half = [(0, ((k, f), (k, f + 1))) for f in (2, 0) for k in (0, 1)]
+    first_half = [(0, ((0, f), (0, f + 1), (1, f), (1, f + 1))) for f in (0, 2)]
     own_place, beside = (1, ((0, 0), (1, 0))), (1, ((0, 1), (0, 3), (1, 1), (1, 3)))
     rings = [(first_half, 2 * b + way, (0, b, d, way)) for d in (2, 1) for b in (0, 1) for way in (0, 1)]
     rings += [(first_half + [own_place], 2 * b + way, (0, b, 0, way)) for b in (0, 1) for way in (0, 1)]

time: 72.7 us -> 72.1 us (level)
  Pallas kernels: 70.1 us -> 69 us
    pallas_call x1, Pallas kernels: 70.1 us -> 69 us  [shards(): pl.pallas_call(functools.partial(kernel, scale, panel, slots, nneg), out_...]
where the time goes in v6:
time: 72.1 us; the launch traced here: 71.5 us
  Pallas kernels  69 us (96%)
  local copies, waits for them, and re-layouts  1.82 us (3%)
    pallas_call x1, Pallas kernels, shards(): pl.pallas_call(functools.partial(kernel, scale, panel, slots, nneg), out_...  69 us
    unnamed x2, local copies, waits for them, and re-layouts  1.82 us

profile of v6, /device:TPU:32, one launch (start us, length us, event | category | flops | bytes accessed | tf_op | source)
XLA Modules:
  0.0 71.5 jit_solution(15165085779848247252)
XLA Ops:
  0.6 69.0 %step.1 = (f32[64,768]{1,0:T(8,128)S(1)}, f32[512,768]{1,0:T(8,128)S(1)}) custom-call(bf16[512,768]{1,0:T(8,128)(2,1)} %emb_hbm.1, f32[64,768]{1,0:T(8,128)} %cls_ref.1, s32[1,64]{1,0:T(1,128)} %bitcast.11, s32[4,512]{1,0:T(4,128)} %bitcast.8, s32[4,512]{1,0:T(4,128)} %bitcast.9, s32[4,512]{1,0:T(4,128)} %bitcast.10, s32[32,512]{1,0:T(8,128)} %bitcast.7), custom_call_target="tpu_custom_call" | custom-call | tf_op jit(solution)/shard_map/step/pallas_call | solution.py:461
  69.6 0.7 copy.11
  70.3 1.1 %copy.12 = f32[512,768]{1,0:T(8,128)} copy(f32[512,768]{1,0:T(8,128)S(1)} %get-tuple-element.3) | data formatting | bytes 3145728

commit v7 on v6

--- a/solution.py
+++ b/solution.py
@@ -425,14 +425,14 @@
     second_sends(0)
     second_sends(1)
     second_relays(0)
-    returned.wait_recv()
-    eg_ref[...] = eg[pl.ds(0, docs), :] + eg_in[...]
     second_relays(1)
     plane_sum(0)
     z_sends(0)
     plane_sum(1)
     z_sends(1)
 
+    returned.wait_recv()
+    eg_ref[...] = eg[pl.ds(0, docs), :] + eg_in[...]
     total = V[0, at.e]
     for k, copy in enumerate(slices):
         copy.wait_recv()

time: 72.1 us -> 72.1 us (level)
  no operation moved by 1% of the time
where the time goes in v7:
time: 72.1 us; the launch traced here: 71.5 us
  Pallas kernels  69 us (96%)
  local copies, waits for them, and re-layouts  1.82 us (3%)
    pallas_call x1, Pallas kernels, shards(): pl.pallas_call(functools.partial(kernel, scale, panel, slots, nneg), out_...  69 us
    unnamed x2, local copies, waits for them, and re-layouts  1.82 us

profile of v7, /device:TPU:32, one launch (start us, length us, event | category | flops | bytes accessed | tf_op | source)
XLA Modules:
  0.0 71.5 jit_solution(15951986629442802097)
XLA Ops:
  0.6 69.0 %step.1 = (f32[64,768]{1,0:T(8,128)S(1)}, f32[512,768]{1,0:T(8,128)S(1)}) custom-call(bf16[512,768]{1,0:T(8,128)(2,1)} %emb_hbm.1, f32[64,768]{1,0:T(8,128)} %cls_ref.1, s32[1,64]{1,0:T(1,128)} %bitcast.11, s32[4,512]{1,0:T(4,128)} %bitcast.8, s32[4,512]{1,0:T(4,128)} %bitcast.9, s32[4,512]{1,0:T(4,128)} %bitcast.10, s32[32,512]{1,0:T(8,128)} %bitcast.7), custom_call_target="tpu_custom_call" | custom-call | tf_op jit(solution)/shard_map/step/pallas_call | solution.py:461
  69.6 0.7 copy.11
  70.3 1.1 %copy.12 = f32[512,768]{1,0:T(8,128)} copy(f32[512,768]{1,0:T(8,128)S(1)} %get-tuple-element.3) | data formatting | bytes 3145728
